TPU v7x, 32 devices: a whole 2x2x4 slice. The times are simulated.
32 devices in a mesh: rows: 8 (over z, y), cols: 4 (over x, core).
Axes of the slice: x: 2, y: 2, z: 4, core: 2. Of those that a mesh axis runs over, the one named last changes fastest.
Arguments:
- sketches: bfloat16 [2048, 16384], P('rows', 'cols'), may hold values from -6 to 6, as said below
- start_basis: bfloat16 [16384, 256], P('cols'), may hold values from -6 to 6
- shrink_index: int32 [1], replicated, may hold values from 64 to 191
Outputs:
- shrunk: float32 [256, 16384], P('rows', 'cols')
Inputs may be any that keep to these rules, and one draw needn't show every extreme that they name: `sketches`: real entries.
All inputs are finite; a program needn't handle non-finite values.
Results may differ from a plain program's by a relative error of at most 0.0028.
Values may be sent and summed in bfloat16 or wider, within the bound.
A program may use at most 64 MiB of HBM per device.

v0:
```python
import jax
import jax.numpy as jnp
from jax import lax
from jax.sharding import PartitionSpec as P

ITERS = 3


def project(sketches, basis_bf):
    partial_product = jnp.dot(sketches, basis_bf, preferred_element_type=jnp.float32)
    return lax.psum(partial_product, "cols")


def orthonormal(images, gram_total):
    lower_factor = jnp.linalg.cholesky(gram_total)
    return jax.scipy.linalg.solve_triangular(lower_factor, images.T, lower=True).T


def body(sketches, start_basis, shrink_index):
    basis_bf = start_basis
    basis = start_basis.astype(jnp.float32)
    for loop_index in range(ITERS):
        projected_bf = project(sketches, basis_bf).astype(jnp.bfloat16)
        local_images = jnp.einsum(
            "lw,lk->wk", sketches, projected_bf, preferred_element_type=jnp.float32
        )
        images = lax.psum(local_images, "rows")
        gram_total = lax.psum(jnp.dot(images.T, images, precision=lax.Precision.HIGHEST), "cols")
        basis = orthonormal(images, gram_total)
        basis_bf = basis.astype(jnp.bfloat16)
    projected = project(sketches, basis_bf)
    energy = lax.psum(jnp.sum(projected * projected, axis=0), "rows")
    ordered = jnp.sort(energy)[::-1]
    threshold = lax.dynamic_index_in_dim(ordered, shrink_index[0], 0, keepdims=False)
    factor = jnp.sqrt(jnp.maximum(energy - threshold, 0.25 * threshold))
    owned_rows = basis.shape[1] // lax.axis_size("rows")
    offset = lax.axis_index("rows") * owned_rows
    columns = lax.dynamic_slice_in_dim(basis, offset, owned_rows, 1)
    scaled = columns * lax.dynamic_slice_in_dim(factor, offset, owned_rows, 0)[None, :]
    return scaled.T


def solution(mesh):
    return jax.shard_map(
        body,
        mesh=mesh,
        in_specs=(P("rows", "cols"), P("cols", None), P()),
        out_specs=P("rows", "cols"),
        check_vma=False,
    )
```

profile of v0, /device:TPU:0, one launch (start us, length us, event | category | flops | bytes accessed | tf_op | source)
XLA Modules:
  0.0 932.8 jit_solution(5308531713813557644)
XLA Ops:
  6.5 1.6 copy-done
  8.1 2.3 fusion.53
  10.4 16.3 %all-reduce.25 = bf16[256,256]{1,0:T(8,128)(2,1)S(1)} all-reduce(f32[256,256]{1,0:T(8,128)S(1)} %fusion.53), channel_id=1, replica_groups=mesh['rows'=8,'cols'=4] {'cols'}, use_global_device_ids=true, to_apply=%region_0.0 | all-reduce | flops 65536 | bytes 393216 | tf_op jit(solution)/shard_map/psum | solution.py:11
  26.7 2.7 convolution_bitcast_fusion.2
  29.5 157.0 %all-reduce.12.cloned.1.call-done = f32[4096,256]{0,1:T(8,128)} async-done(((f32[4096,256]{0,1:T(8,128)}), f32[4096,256]{0,1:T(8,128)}) %all-reduce.12.cloned.1.call-update) | async-done | bytes 4194320 | tf_op jit(solution)/shard_map/psum | solution.py:27
  186.5 7.7 fusion.54
  194.7 30.9 %all-reduce.14.cloned.1.call-done = f32[256,256]{0,1:T(8,128)} async-done(((f32[256,256]{0,1:T(8,128)}), f32[256,256]{0,1:T(8,128)}) %all-reduce.14.cloned.1.call-update) | async-done | bytes 262160 | tf_op jit(solution)/shard_map/psum | solution.py:28
  225.6 1.1 copy.5
  226.7 1.0 fusion.20
  227.7 11.7 %cholesky.172 = f32[128,128]{1,0:T(8,128)S(1)} custom-call(f32[128,128]{1,0:T(8,128)S(1)} %cholesky.270), custom_call_target="Cholesky" | custom-call | tf_op jit(solution)/shard_map/jit(cholesky)/cholesky | solution.py:15
  239.5 9.8 %custom-call.15 = f32[1,128,128]{1,2,0:T(8,128)S(1)} custom-call(f32[1,128,128]{2,1,0:T(8,128)S(1)} %get-tuple-element.74), custom_call_target="InvertDiagBlocksLowerTriangular" | custom-call | tf_op jit(solution)/shard_map/jit(cholesky)/cholesky | solution.py:15
  249.8 11.7 %cholesky.189 = f32[128,128]{1,0:T(8,128)S(1)} custom-call(f32[128,128]{1,0:T(8,128)S(1)} %convolution_subtract_fusion.5), custom_call_target="Cholesky" | custom-call | tf_op jit(solution)/shard_map/jit(cholesky)/cholesky | solution.py:15
  261.5 0.7 compare_reduce_fusion.4
  263.6 4.1 while.6
  264.4 1.4 bitcast_dynamic-update-slice_fusion.6
  266.3 1.4 bitcast_dynamic-update-slice_fusion.6
  267.7 19.7 %custom-call.16 = f32[2,128,128]{1,2,0:T(8,128)S(1)} custom-call(f32[2,128,128]{2,1,0:T(8,128)S(1)} %get-tuple-element.30), custom_call_target="InvertDiagBlocksLowerTriangular" | custom-call | tf_op jit(solution)/shard_map/jit(_solve_triangular)/triangular_solve | solution.py:16
  287.4 3.6 fusion.9
  291.1 2.0 convolution_subtract_fusion.2
  293.1 1.9 fusion.33
  295.0 0.9 fusion.14
  295.9 13.5 %all-reduce.26 = bf16[256,256]{0,1:T(8,128)(2,1)S(1)} all-reduce(f32[256,256]{0,1:T(8,128)S(1)} %fusion.14), channel_id=1, replica_groups=mesh['rows'=8,'cols'=4] {'cols'}, use_global_device_ids=true, to_apply=%region_7.0 | all-reduce | flops 65536 | bytes 393216 | tf_op jit(solution)/shard_map/psum | solution.py:11
  309.4 2.7 convolution_bitcast_fusion.1
  312.1 156.6 %all-reduce.16.cloned.1.call-done = f32[4096,256]{0,1:T(8,128)} async-done(((f32[4096,256]{0,1:T(8,128)}), f32[4096,256]{0,1:T(8,128)}) %all-reduce.16.cloned.1.call-update) | async-done | bytes 4194320 | tf_op jit(solution)/shard_map/psum | solution.py:27
  468.7 7.7 fusion.55
  476.9 31.0 %all-reduce.18.cloned.1.call-done = f32[256,256]{0,1:T(8,128)} async-done(((f32[256,256]{0,1:T(8,128)}), f32[256,256]{0,1:T(8,128)}) %all-reduce.18.cloned.1.call-update) | async-done | bytes 262160 | tf_op jit(solution)/shard_map/psum | solution.py:28
  507.9 1.1 copy.7
  508.9 1.0 fusion.19
  509.9 11.7 %cholesky.206 = f32[128,128]{1,0:T(8,128)S(1)} custom-call(f32[128,128]{1,0:T(8,128)S(1)} %cholesky.273), custom_call_target="Cholesky" | custom-call | tf_op jit(solution)/shard_map/jit(cholesky)/cholesky | solution.py:15
  521.7 9.8 %custom-call.17 = f32[1,128,128]{1,2,0:T(8,128)S(1)} custom-call(f32[1,128,128]{2,1,0:T(8,128)S(1)} %get-tuple-element.70), custom_call_target="InvertDiagBlocksLowerTriangular" | custom-call | tf_op jit(solution)/shard_map/jit(cholesky)/cholesky | solution.py:15
  532.0 11.7 %cholesky.223 = f32[128,128]{1,0:T(8,128)S(1)} custom-call(f32[128,128]{1,0:T(8,128)S(1)} %convolution_subtract_fusion.4), custom_call_target="Cholesky" | custom-call | tf_op jit(solution)/shard_map/jit(cholesky)/cholesky | solution.py:15
  546.4 4.1 while.7
  547.2 1.4 bitcast_dynamic-update-slice_fusion.7
  549.1 1.4 bitcast_dynamic-update-slice_fusion.7
  550.5 19.7 %custom-call.18 = f32[2,128,128]{1,2,0:T(8,128)S(1)} custom-call(f32[2,128,128]{2,1,0:T(8,128)S(1)} %get-tuple-element.31), custom_call_target="InvertDiagBlocksLowerTriangular" | custom-call | tf_op jit(solution)/shard_map/jit(_solve_triangular)/triangular_solve | solution.py:16
  570.2 3.6 fusion.7
  573.8 2.0 convolution_subtract_fusion.1
  575.8 1.9 fusion.29
  577.8 0.9 fusion.15
  578.7 13.5 %all-reduce.27 = bf16[256,256]{0,1:T(8,128)(2,1)S(1)} all-reduce(f32[256,256]{0,1:T(8,128)S(1)} %fusion.15), channel_id=1, replica_groups=mesh['rows'=8,'cols'=4] {'cols'}, use_global_device_ids=true, to_apply=%region_10.0 | all-reduce | flops 65536 | bytes 393216 | tf_op jit(solution)/shard_map/psum | solution.py:11
  592.2 2.7 convolution_bitcast_fusion
  594.9 156.5 %all-reduce.20.cloned.1.call-done = f32[4096,256]{0,1:T(8,128)} async-done(((f32[4096,256]{0,1:T(8,128)}), f32[4096,256]{0,1:T(8,128)}) %all-reduce.20.cloned.1.call-update) | async-done | bytes 4194320 | tf_op jit(solution)/shard_map/psum | solution.py:27
  751.5 7.7 fusion.56
  759.4 31.2 %all-reduce.22.cloned.1.call-done = f32[256,256]{0,1:T(8,128)} async-done(((f32[256,256]{0,1:T(8,128)}), f32[256,256]{0,1:T(8,128)}) %all-reduce.22.cloned.1.call-update) | async-done | bytes 262160 | tf_op jit(solution)/shard_map/psum | solution.py:28
  790.6 1.1 copy.9
  791.7 1.0 fusion.18
  792.7 11.7 %cholesky.240 = f32[128,128]{1,0:T(8,128)S(1)} custom-call(f32[128,128]{1,0:T(8,128)S(1)} %cholesky.276), custom_call_target="Cholesky" | custom-call | tf_op jit(solution)/shard_map/jit(cholesky)/cholesky | solution.py:15
  804.5 9.8 %custom-call.19 = f32[1,128,128]{1,2,0:T(8,128)S(1)} custom-call(f32[1,128,128]{2,1,0:T(8,128)S(1)} %get-tuple-element.66), custom_call_target="InvertDiagBlocksLowerTriangular" | custom-call | tf_op jit(solution)/shard_map/jit(cholesky)/cholesky | solution.py:15
  814.8 11.7 %cholesky.257 = f32[128,128]{1,0:T(8,128)S(1)} custom-call(f32[128,128]{1,0:T(8,128)S(1)} %convolution_subtract_fusion.3), custom_call_target="Cholesky" | custom-call | tf_op jit(solution)/shard_map/jit(cholesky)/cholesky | solution.py:15
  829.1 4.2 while.8
  830.0 1.4 bitcast_dynamic-update-slice_fusion.8
  832.0 1.4 bitcast_dynamic-update-slice_fusion.8
  833.3 19.7 %custom-call.20 = f32[2,128,128]{1,2,0:T(8,128)S(1)} custom-call(f32[2,128,128]{2,1,0:T(8,128)S(1)} %get-tuple-element.32), custom_call_target="InvertDiagBlocksLowerTriangular" | custom-call | tf_op jit(solution)/shard_map/jit(_solve_triangular)/triangular_solve | solution.py:16
  853.0 3.6 fusion.5
  856.7 1.9 convolution_subtract_fusion
  858.6 1.9 fusion.25
  860.6 1.3 copy-done.5
  861.9 1.5 fusion.11
  864.0 31.8 %all-reduce.24.cloned.1.call-done = f32[256,256]{0,1:T(8,128)} async-done(((f32[256,256]{0,1:T(8,128)}), f32[256,256]{0,1:T(8,128)}) %all-reduce.24.cloned.1.call-update) | async-done | bytes 262160 | tf_op jit(solution)/shard_map/psum | solution.py:11
  895.8 1.1 multiply_reduce_fusion
  896.9 21.4 %psum.87 = f32[256]{0:T(256)S(1)} all-reduce(f32[256]{0:T(256)S(1)} %multiply_reduce_fusion), channel_id=1, replica_groups=mesh['rows'=8,'cols'=4] {'rows'}, use_global_device_ids=true, to_apply=%region_15.18 | all-reduce | flops 256 | bytes 2048 | tf_op jit(solution)/shard_map/psum | solution.py:32
  918.3 3.3 sort.15
  922.9 0.7 maximum_sqrt_fusion
  923.6 1.9 fusion.17
  (70 shorter events, 10.2 us)
Async XLA Ops:
  6.5 1.6 copy-start
  6.5 179.9 %all-reduce.12.cloned.1.call-start = ((), (), s32[]{:S(2)}) async-start(), calls=%async_computation | async-start | bytes 8388608 | tf_op jit(solution)/shard_map/psum | solution.py:27
  29.4 196.2 %all-reduce.14.cloned.1.call-start = ((), (), s32[]{:S(2)}) async-start(), calls=%async_computation.1 | async-start | bytes 524288 | tf_op jit(solution)/shard_map/psum | solution.py:28
  194.2 274.5 %all-reduce.16.cloned.1.call-start = ((), (), s32[]{:S(2)}) async-start(), calls=%async_computation.2 | async-start | bytes 8388608 | tf_op jit(solution)/shard_map/psum | solution.py:27
  287.4 3.7 copy-start.1
  312.1 195.8 %all-reduce.18.cloned.1.call-start = ((), (), s32[]{:S(2)}) async-start(), calls=%async_computation.3 | async-start | bytes 524288 | tf_op jit(solution)/shard_map/psum | solution.py:28
  476.4 275.0 %all-reduce.20.cloned.1.call-start = ((), (), s32[]{:S(2)}) async-start(), calls=%async_computation.4 | async-start | bytes 8388608 | tf_op jit(solution)/shard_map/psum | solution.py:27
  570.2 3.7 copy-start.3
  594.9 195.7 %all-reduce.22.cloned.1.call-start = ((), (), s32[]{:S(2)}) async-start(), calls=%async_computation.5 | async-start | bytes 524288 | tf_op jit(solution)/shard_map/psum | solution.py:28
  759.2 136.6 %all-reduce.24.cloned.1.call-start = ((), (), s32[]{:S(2)}) async-start(), calls=%async_computation.6 | async-start | bytes 524288 | tf_op jit(solution)/shard_map/psum | solution.py:11
  853.0 3.7 copy-start.2
  856.7 3.9 copy-start.4
  860.6 1.3 copy-start.5
Sparse Core Ops, SparseCore 0:
  29.6 156.8 all-reduce.11
  194.3 31.2 all-reduce.13
  312.2 156.4 all-reduce.15
  476.5 31.2 all-reduce.17
  595.0 156.4 all-reduce.19
  759.3 31.2 all-reduce.21
  863.5 32.2 all-reduce.23
where the time goes:
time: 938 us; the launch traced here: 933 us
  waiting for transfers between devices  595 us (63%)
  other arithmetic  172 us (18%)
  blocking collectives  64.6 us (7%)
  matrix products  60.7 us (6%)
  between operations  19.5 us (2%)
  local copies, waits for them, and re-layouts  18.7 us (2%)
    psum x3, waiting for transfers between devices, body(): images = lax.psum(local_images, 'rows')  470 us
    another operation x20, other arithmetic, orthonormal(): lower_factor = jnp.linalg.cholesky(gram_total)  103 us
    psum x3, waiting for transfers between devices, body(): lax.psum(jnp.dot(images.T, images, precision=lax.Precision.HIGHEST), 'cols')  93 us
    another operation x7, other arithmetic, orthonormal(): jax.scipy.linalg.solve_triangular(lower_factor, images.T, lower=True)  59.1 us
    psum x3, blocking collectives, project(): return lax.psum(partial_product, 'cols')  43.3 us
    psum x1, waiting for transfers between devices, project(): return lax.psum(partial_product, 'cols')  31.8 us
    dot_general x3, matrix products, body(): jnp.dot(images.T, images, precision=lax.Precision.HIGHEST)  23.1 us
    another operation x9, matrix products, orthonormal(): jax.scipy.linalg.solve_triangular(lower_factor, images.T, lower=True)  22.6 us
  transfers between devices with their start and end apart: 7, of which 7 were waited for; matrix products, arithmetic and copies ran while one was open for 0% of the time, Pallas kernels for 0%

commit v1 on v0

--- a/solution.py
+++ b/solution.py
@@ -24,7 +24,11 @@
         local_images = jnp.einsum(
             "lw,lk->wk", sketches, projected_bf, preferred_element_type=jnp.float32
         )
-        images = lax.psum(local_images, "rows")
+        n_dev = lax.axis_size("rows")
+        images, reach = (local_images, 1)
+        while reach < n_dev:
+            images = images + lax.ppermute(images, "rows", [(i, i ^ reach) for i in range(n_dev)])
+            reach = 2 * reach
         gram_total = lax.psum(jnp.dot(images.T, images, precision=lax.Precision.HIGHEST), "cols")
         basis = orthonormal(images, gram_total)
         basis_bf = basis.astype(jnp.bfloat16)

time: 938 us -> 1580 us (1.68)
  waiting for transfers between devices: 595 us -> 1190 us
  other arithmetic: 172 us -> 200 us
  starting transfers between devices: 1.33 us -> 17.9 us
    ppermute x0 -> x9, waiting for transfers between devices: none -> 1070 us  [body(): lax.ppermute(images, 'rows', [(i, i ^ reach) for i in range(n_dev)])]
    psum x3 -> x0, waiting for transfers between devices: 470 us -> none  [body(): images = lax.psum(local_images, 'rows')]
    transpose x0 -> x3, other arithmetic: none -> 18.3 us  [body(): gram_total = lax.psum(jnp.dot(images.T, images, precision=lax.Precision.H...]
    ppermute x0 -> x9, starting transfers between devices: none -> 17.2 us  [body(): lax.ppermute(images, 'rows', [(i, i ^ reach) for i in range(n_dev)])]
  transfers between devices with their start and end apart: 7 -> 13, of which waited for: 7 -> 13; matrix products, arithmetic and copies ran while one was open for 0% -> 1% of each run, Pallas kernels for 0% -> 0%
where the time goes in v1:
time: 1580 us
  waiting for transfers between devices  1190 us (75%)
  other arithmetic  200 us (13%)
  blocking collectives  64.6 us (4%)
  matrix products  62.1 us (4%)
  local copies, waits for them, and re-layouts  20 us (1%)
  between operations  18.8 us (1%)
  starting transfers between devices  17.9 us (1%)
    ppermute x9, waiting for transfers between devices, body(): lax.ppermute(images, 'rows', [(i, i ^ reach) for i in range(n_dev)])  1070 us
    another operation x20, other arithmetic, orthonormal(): lower_factor = jnp.linalg.cholesky(gram_total)  103 us
    psum x3, waiting for transfers between devices, body(): lax.psum(jnp.dot(images.T, images, precision=lax.Precision.HIGHEST), 'cols')  92.4 us
    another operation x7, other arithmetic, orthonormal(): jax.scipy.linalg.solve_triangular(lower_factor, images.T, lower=True)  59.1 us
    psum x3, blocking collectives, project(): return lax.psum(partial_product, 'cols')  43.3 us
    psum x1, waiting for transfers between devices, project(): return lax.psum(partial_product, 'cols')  31.8 us
  transfers between devices with their start and end apart: 13, of which 13 were waited for; matrix products, arithmetic and copies ran while one was open for 1% of the time, Pallas kernels for 0%

profile of v1, /device:TPU:0, one launch (start us, length us, event | category | flops | bytes accessed | tf_op | source)
XLA Modules:
  0.0 1578.1 jit_solution(3236673249336293420)
XLA Ops:
  6.5 1.6 copy-done
  8.1 2.3 fusion.62
  10.4 16.3 %all-reduce.16 = bf16[256,256]{1,0:T(8,128)(2,1)S(1)} all-reduce(f32[256,256]{1,0:T(8,128)S(1)} %fusion.62), channel_id=1, replica_groups=mesh['rows'=8,'cols'=4] {'cols'}, use_global_device_ids=true, to_apply=%region_0.0 | all-reduce | flops 65536 | bytes 393216 | tf_op jit(solution)/shard_map/psum | solution.py:11
  27.4 1.6 collective-permute-start
  29.0 89.6 %collective-permute-done = f32[4096,256]{0,1:T(8,128)S(1)} collective-permute-done((f32[4096,256]{0,1:T(8,128)S(1)}, f32[4096,256]{0,1:T(8,128)S(1)}, u32[]{:S(2)}, u32[]{:S(2)}) %collective-permute-start) | collective-permute-done | bytes 4194336 | tf_op jit(solution)/shard_map/ppermute | solution.py:30
  119.2 1.9 collective-permute-start.1
  121.1 88.7 %collective-permute-done.1 = f32[4096,256]{0,1:T(8,128)S(1)} collective-permute-done((f32[4096,256]{0,1:T(8,128)S(1)}, f32[4096,256]{0,1:T(8,128)S(1)}, u32[]{:S(2)}, u32[]{:S(2)}) %collective-permute-start.1) | collective-permute-done | bytes 4194336 | tf_op jit(solution)/shard_map/ppermute | solution.py:30
  209.8 2.5 add.70
  212.3 2.7 collective-permute-start.2
  215.0 178.0 %collective-permute-done.2 = f32[4096,256]{0,1:T(8,128)} collective-permute-done((f32[4096,256]{0,1:T(8,128)}, f32[4096,256]{0,1:T(8,128)}, u32[]{:S(2)}, u32[]{:S(2)}) %collective-permute-start.2) | collective-permute-done | bytes 4194336 | tf_op jit(solution)/shard_map/ppermute | solution.py:30
  393.0 10.4 fusion.18
  403.6 6.1 add_bitcast_fusion.2
  409.7 30.5 %all-reduce.9.cloned.1.call-done = f32[256,256]{0,1:T(8,128)} async-done(((f32[256,256]{0,1:T(8,128)}), f32[256,256]{0,1:T(8,128)}) %all-reduce.9.cloned.1.call-update) | async-done | bytes 262160 | tf_op jit(solution)/shard_map/psum | solution.py:32
  442.3 11.7 cholesky.172
  454.1 9.8 custom-call.15
  464.4 11.7 cholesky.189
  478.1 4.3 while.6
  482.4 19.7 %custom-call.16 = f32[2,128,128]{1,2,0:T(8,128)S(1)} custom-call(f32[2,128,128]{2,1,0:T(8,128)S(1)} %get-tuple-element.30), custom_call_target="InvertDiagBlocksLowerTriangular" | custom-call | tf_op jit(solution)/shard_map/jit(_solve_triangular)/triangular_solve | solution.py:16
  502.1 3.5 fusion.12
  505.6 1.9 fusion.41
  507.8 2.0 fusion.11
  510.5 13.5 all-reduce.17
  524.7 1.6 collective-permute-start.3
  526.3 89.6 %collective-permute-done.3 = f32[4096,256]{0,1:T(8,128)S(1)} collective-permute-done((f32[4096,256]{0,1:T(8,128)S(1)}, f32[4096,256]{0,1:T(8,128)S(1)}, u32[]{:S(2)}, u32[]{:S(2)}) %collective-permute-start.3) | collective-permute-done | bytes 4194336 | tf_op jit(solution)/shard_map/ppermute | solution.py:30
  616.6 1.6 collective-permute-start.4
  618.2 88.8 %collective-permute-done.4 = f32[4096,256]{0,1:T(8,128)S(1)} collective-permute-done((f32[4096,256]{0,1:T(8,128)S(1)}, f32[4096,256]{0,1:T(8,128)S(1)}, u32[]{:S(2)}, u32[]{:S(2)}) %collective-permute-start.4) | collective-permute-done | bytes 4194336 | tf_op jit(solution)/shard_map/ppermute | solution.py:30
  707.0 2.5 add.73
  709.5 2.4 collective-permute-start.5
  711.9 178.2 %collective-permute-done.5 = f32[4096,256]{0,1:T(8,128)} collective-permute-done((f32[4096,256]{0,1:T(8,128)}, f32[4096,256]{0,1:T(8,128)}, u32[]{:S(2)}, u32[]{:S(2)}) %collective-permute-start.5) | collective-permute-done | bytes 4194336 | tf_op jit(solution)/shard_map/ppermute | solution.py:30
  890.1 10.4 fusion.16
  900.7 6.1 add_bitcast_fusion.1
  906.8 31.0 %all-reduce.11.cloned.1.call-done = f32[256,256]{0,1:T(8,128)} async-done(((f32[256,256]{0,1:T(8,128)}), f32[256,256]{0,1:T(8,128)}) %all-reduce.11.cloned.1.call-update) | async-done | bytes 262160 | tf_op jit(solution)/shard_map/psum | solution.py:32
  939.8 11.7 cholesky.206
  951.6 9.8 custom-call.17
  961.9 11.7 cholesky.223
  976.2 4.3 while.7
  980.4 19.7 %custom-call.18 = f32[2,128,128]{1,2,0:T(8,128)S(1)} custom-call(f32[2,128,128]{2,1,0:T(8,128)S(1)} %get-tuple-element.31), custom_call_target="InvertDiagBlocksLowerTriangular" | custom-call | tf_op jit(solution)/shard_map/jit(_solve_triangular)/triangular_solve | solution.py:16
  1000.1 3.5 fusion.9
  1003.6 1.9 fusion.37
  1005.8 2.0 fusion.8
  1008.6 13.5 all-reduce.18
  1022.8 1.6 collective-permute-start.6
  1024.4 89.6 %collective-permute-done.6 = f32[4096,256]{0,1:T(8,128)S(1)} collective-permute-done((f32[4096,256]{0,1:T(8,128)S(1)}, f32[4096,256]{0,1:T(8,128)S(1)}, u32[]{:S(2)}, u32[]{:S(2)}) %collective-permute-start.6) | collective-permute-done | bytes 4194336 | tf_op jit(solution)/shard_map/ppermute | solution.py:30
  1114.7 1.6 collective-permute-start.7
  1116.2 88.8 %collective-permute-done.7 = f32[4096,256]{0,1:T(8,128)S(1)} collective-permute-done((f32[4096,256]{0,1:T(8,128)S(1)}, f32[4096,256]{0,1:T(8,128)S(1)}, u32[]{:S(2)}, u32[]{:S(2)}) %collective-permute-start.7) | collective-permute-done | bytes 4194336 | tf_op jit(solution)/shard_map/ppermute | solution.py:30
  1205.1 2.5 add.76
  1207.5 2.4 collective-permute-start.8
  1209.9 178.2 %collective-permute-done.8 = f32[4096,256]{0,1:T(8,128)} collective-permute-done((f32[4096,256]{0,1:T(8,128)}, f32[4096,256]{0,1:T(8,128)}, u32[]{:S(2)}, u32[]{:S(2)}) %collective-permute-start.8) | collective-permute-done | bytes 4194336 | tf_op jit(solution)/shard_map/ppermute | solution.py:30
  1388.1 10.4 fusion.14
  1398.7 6.1 add_bitcast_fusion
  1404.8 31.0 %all-reduce.13.cloned.1.call-done = f32[256,256]{0,1:T(8,128)} async-done(((f32[256,256]{0,1:T(8,128)}), f32[256,256]{0,1:T(8,128)}) %all-reduce.13.cloned.1.call-update) | async-done | bytes 262160 | tf_op jit(solution)/shard_map/psum | solution.py:32
  1437.9 11.7 cholesky.240
  1449.6 9.8 custom-call.19
  1459.9 11.7 cholesky.257
  1474.2 4.1 while.8
  1478.3 19.7 %custom-call.20 = f32[2,128,128]{1,2,0:T(8,128)S(1)} custom-call(f32[2,128,128]{2,1,0:T(8,128)S(1)} %get-tuple-element.32), custom_call_target="InvertDiagBlocksLowerTriangular" | custom-call | tf_op jit(solution)/shard_map/jit(_solve_triangular)/triangular_solve | solution.py:16
  1498.0 3.5 fusion.6
  1501.5 1.9 fusion.33
  1504.4 2.0 fusion.5
  1507.7 1.5 fusion.20
  1509.9 31.8 %all-reduce.15.cloned.1.call-done = f32[256,256]{0,1:T(8,128)} async-done(((f32[256,256]{0,1:T(8,128)}), f32[256,256]{0,1:T(8,128)}) %all-reduce.15.cloned.1.call-update) | async-done | bytes 262160 | tf_op jit(solution)/shard_map/psum | solution.py:11
  1542.7 21.4 %psum.63 = f32[256]{0:T(256)S(1)} all-reduce(f32[256]{0:T(256)S(1)} %multiply_reduce_fusion), channel_id=1, replica_groups=mesh['rows'=8,'cols'=4] {'rows'}, use_global_device_ids=true, to_apply=%region_12.15 | all-reduce | flops 256 | bytes 2048 | tf_op jit(solution)/shard_map/psum | solution.py:36
  1564.1 3.3 sort.15
  1569.4 1.9 fusion.26
  (88 shorter events, 34.3 us)
Async XLA Ops:
  6.5 1.6 copy-start
  6.5 433.7 %all-reduce.9.cloned.1.call-start = ((), (), s32[]{:S(2)}) async-start(), calls=%async_computation | async-start | bytes 524288 | tf_op jit(solution)/shard_map/psum | solution.py:32
  27.4 91.1 %collective-permute-start = (f32[4096,256]{0,1:T(8,128)S(1)}, f32[4096,256]{0,1:T(8,128)S(1)}, u32[]{:S(2)}, u32[]{:S(2)}) collective-permute-start(f32[4096,256]{0,1:T(8,128)S(1)} %convolution_bitcast_fusion.2), channel_id=1, source_target_pairs={{0,4},{4,0},{8,12},{12,8},{16,20},{20,16},{24,28},{28,24},{1,5},{5... | collective-permute-start | bytes 12582920 | tf_op jit(solution)/shard_map/ppermute | solution.py:30
  119.2 90.6 %collective-permute-start.1 = (f32[4096,256]{0,1:T(8,128)S(1)}, f32[4096,256]{0,1:T(8,128)S(1)}, u32[]{:S(2)}, u32[]{:S(2)}) collective-permute-start(f32[4096,256]{0,1:T(8,128)S(1)} %add.69), channel_id=1, source_target_pairs={{0,8},{4,12},{8,0},{12,4},{16,24},{20,28},{24,16},{28,20},{1,9},{5... | collective-permute-start | bytes 12582920 | tf_op jit(solution)/shard_map/ppermute | solution.py:30
  212.3 180.8 %collective-permute-start.2 = (f32[4096,256]{0,1:T(8,128)}, f32[4096,256]{0,1:T(8,128)}, u32[]{:S(2)}, u32[]{:S(2)}) collective-permute-start(f32[4096,256]{0,1:T(8,128)} %add.70), channel_id=1, source_target_pairs={{0,16},{4,20},{8,24},{12,28},{16,0},{20,4},{24,8},{28,12},{1,17},{... | collective-permute-start | bytes 12582920 | tf_op jit(solution)/shard_map/ppermute | solution.py:30
  403.4 534.3 %all-reduce.11.cloned.1.call-start = ((), (), s32[]{:S(2)}) async-start(), calls=%async_computation.1 | async-start | bytes 524288 | tf_op jit(solution)/shard_map/psum | solution.py:32
  505.6 2.2 copy-start.4
  524.7 91.2 %collective-permute-start.3 = (f32[4096,256]{0,1:T(8,128)S(1)}, f32[4096,256]{0,1:T(8,128)S(1)}, u32[]{:S(2)}, u32[]{:S(2)}) collective-permute-start(f32[4096,256]{0,1:T(8,128)S(1)} %convolution_bitcast_fusion.1), channel_id=1, source_target_pairs={{0,4},{4,0},{8,12},{12,8},{16,20},{20,16},{24,28},{28,24},{1,5},{5... | collective-permute-start | bytes 12582920 | tf_op jit(solution)/shard_map/ppermute | solution.py:30
  616.6 90.4 %collective-permute-start.4 = (f32[4096,256]{0,1:T(8,128)S(1)}, f32[4096,256]{0,1:T(8,128)S(1)}, u32[]{:S(2)}, u32[]{:S(2)}) collective-permute-start(f32[4096,256]{0,1:T(8,128)S(1)} %add.72), channel_id=1, source_target_pairs={{0,8},{4,12},{8,0},{12,4},{16,24},{20,28},{24,16},{28,20},{1,9},{5... | collective-permute-start | bytes 12582920 | tf_op jit(solution)/shard_map/ppermute | solution.py:30
  709.5 180.6 %collective-permute-start.5 = (f32[4096,256]{0,1:T(8,128)}, f32[4096,256]{0,1:T(8,128)}, u32[]{:S(2)}, u32[]{:S(2)}) collective-permute-start(f32[4096,256]{0,1:T(8,128)} %add.73), channel_id=1, source_target_pairs={{0,16},{4,20},{8,24},{12,28},{16,0},{20,4},{24,8},{28,12},{1,17},{... | collective-permute-start | bytes 12582920 | tf_op jit(solution)/shard_map/ppermute | solution.py:30
  900.5 535.3 %all-reduce.13.cloned.1.call-start = ((), (), s32[]{:S(2)}) async-start(), calls=%async_computation.2 | async-start | bytes 524288 | tf_op jit(solution)/shard_map/psum | solution.py:32
  1003.6 2.2 copy-start.5
  1022.8 91.2 %collective-permute-start.6 = (f32[4096,256]{0,1:T(8,128)S(1)}, f32[4096,256]{0,1:T(8,128)S(1)}, u32[]{:S(2)}, u32[]{:S(2)}) collective-permute-start(f32[4096,256]{0,1:T(8,128)S(1)} %convolution_bitcast_fusion), channel_id=1, source_target_pairs={{0,4},{4,0},{8,12},{12,8},{16,20},{20,16},{24,28},{28,24},{1,5},{5... | collective-permute-start | bytes 12582920 | tf_op jit(solution)/shard_map/ppermute | solution.py:30
  1114.7 90.4 %collective-permute-start.7 = (f32[4096,256]{0,1:T(8,128)S(1)}, f32[4096,256]{0,1:T(8,128)S(1)}, u32[]{:S(2)}, u32[]{:S(2)}) collective-permute-start(f32[4096,256]{0,1:T(8,128)S(1)} %add.75), channel_id=1, source_target_pairs={{0,8},{4,12},{8,0},{12,4},{16,24},{20,28},{24,16},{28,20},{1,9},{5... | collective-permute-start | bytes 12582920 | tf_op jit(solution)/shard_map/ppermute | solution.py:30
  1207.5 180.6 %collective-permute-start.8 = (f32[4096,256]{0,1:T(8,128)}, f32[4096,256]{0,1:T(8,128)}, u32[]{:S(2)}, u32[]{:S(2)}) collective-permute-start(f32[4096,256]{0,1:T(8,128)} %add.76), channel_id=1, source_target_pairs={{0,16},{4,20},{8,24},{12,28},{16,0},{20,4},{24,8},{28,12},{1,17},{... | collective-permute-start | bytes 12582920 | tf_op jit(solution)/shard_map/ppermute | solution.py:30
  1398.5 143.1 %all-reduce.15.cloned.1.call-start = ((), (), s32[]{:S(2)}) async-start(), calls=%async_computation.3 | async-start | bytes 524288 | tf_op jit(solution)/shard_map/psum | solution.py:11
  1501.5 4.9 copy-start.1
  1501.5 2.9 copy-start.3
  1506.4 1.3 copy-start.2
Sparse Core Ops, SparseCore 0:
  403.5 36.6 all-reduce.8
  900.6 37.1 all-reduce.10
  1398.6 37.1 all-reduce.12
  1509.3 32.2 all-reduce.14
